TPU v7x, 256 devices: a whole 4x4x8 slice. The times are simulated.
256 devices in a mesh: row: 4 (over z_lo, core), col: 16 (over y, x), depth: 4 (over z_hi).
Axes of the slice: x: 4, y: 4, z: 8 (z_hi: 4, z_lo: 2; z = z_hi * 2 + z_lo), core: 2. Of those that a mesh axis runs over, the one named last changes fastest.
Arguments:
- diag_two: float32 [256, 256], replicated, may hold values from -3 to 3, as said below
- diag_one: float32 [256, 256], replicated, may hold values from -3 to 3, as said below
- cross_tile: float32 [256, 256], replicated, may hold values from -0.375 to 0.375
- left_two: float32 [256, 32768], P(None, ('col', 'depth')), may hold values from -0.375 to 0.375
- left_one: float32 [256, 32768], P(None, ('col', 'depth')), may hold values from -0.375 to 0.375
- below_left: float32 [4096, 32768], P('row', ('col', 'depth')), may hold values from -0.09375 to 0.09375
- panel_two: float32 [4096, 256], P('row', 'col'), may hold values from -0.09375 to 0.09375
- panel_one: float32 [4096, 256], P('row', 'col'), may hold values from -0.09375 to 0.09375
- grad_diag_two: float32 [256, 256], replicated, may hold values from -6 to 6
- grad_diag_one: float32 [256, 256], replicated, may hold values from -6 to 6
- grad_cross: float32 [256, 256], replicated, may hold values from -6 to 6
- grad_left_two: float32 [256, 32768], P('row', ('col', 'depth')), may hold values from -6 to 6
- grad_left_one: float32 [256, 32768], P('row', ('col', 'depth')), may hold values from -6 to 6
- grad_below: float32 [4096, 32768], P('row', ('col', 'depth')), may hold values from -6 to 6
- grad_panel_two: float32 [4096, 256], P('row', 'col'), may hold values from -6 to 6
- grad_panel_one: float32 [4096, 256], P('row', 'col'), may hold values from -6 to 6
Outputs:
- out_below: float32 [4096, 32768], P('row', ('col', 'depth'))
- out_left_two: float32 [256, 32768], P('row', ('col', 'depth'))
- out_left_one: float32 [256, 32768], P('row', ('col', 'depth'))
- out_diag_two: float32 [256, 256], replicated
- out_diag_one: float32 [256, 256], replicated
- out_cross: float32 [256, 256], replicated
- out_panel_two: float32 [4096, 256], P('row', 'col')
- out_panel_one: float32 [4096, 256], P('row', 'col')
Inputs may be any that keep to these rules, and one draw needn't show every extreme that they name: `diag_two`: lower triangular; its diagonal lies in 1 to 3. `diag_one`: lower triangular; its diagonal lies in 1 to 3.
All inputs are finite; a program needn't handle non-finite values.
Results may differ from a plain program's by a relative error of at most 0.000071.
Values sent between devices are 32-bit elements; how exact they have to be, the bound alone decides.
No kernel may reach another device: no remote copies, remote signals or barrier semaphores. Data moves between devices by JAX's collectives and lax.ppermute only.
A program may use at most 64 MiB of HBM per device.

v0:
```python
import jax
import jax.numpy as jnp
from jax import lax
from jax.sharding import PartitionSpec as P


def gather_turned(arrays, axis, dims):
    turned = [jnp.moveaxis(a, dim, 0) for a, dim in zip(arrays, dims)]
    both = jnp.concatenate([t.reshape(len(t), -1) for t in turned], axis=1)
    out, at, outs = (lax.all_gather(both, axis, axis=0, tiled=True), 0, [])
    for t, dim in zip(turned, dims):
        piece = out[:, at : at + t[0].size].reshape(-1, *t.shape[1:])
        outs.append(jnp.moveaxis(piece, 0, dim))
        at += t[0].size
    return tuple(outs)


def gathered_total(value, axis):
    blocks = lax.all_gather(value, axis)
    return blocks.sum(axis=0)


def sent_to_all(value, axis):
    count = lax.axis_size(axis)
    return lax.all_to_all(
        jnp.broadcast_to(value[None], (count, *value.shape)), axis, 0, 0, tiled=True
    )


def taken_together(value, axis):
    return sent_to_all(value, axis).sum(axis=0)


def in_blocks(value, dim, count):
    before, after = (value.shape[:dim], value.shape[dim + 1 :])
    return jnp.moveaxis(value.reshape(*before, count, -1, *after), dim, 0)


def sum_at_owner(value, axis, dim):
    count = lax.axis_size(axis)
    blocks = lax.all_to_all(in_blocks(value, dim, count), axis, 0, 0, tiled=True)
    return jnp.sum(blocks, axis=0)


def matmul(left, right):
    return jnp.dot(left, right, precision=lax.Precision.HIGHEST, preferred_element_type=jnp.float32)


def right_solve(factor, values):
    return lax.linalg.triangular_solve(factor, values, left_side=False, lower=True)


def halved(square):
    return jnp.tril(square) - 0.5 * jnp.diag(jnp.diag(square))


def reverse_block(factor, cotangent):
    inner = halved(matmul(factor.T, cotangent))
    leftward = lax.linalg.triangular_solve(
        factor, inner, left_side=True, lower=True, transpose_a=True
    )
    spread = right_solve(factor, leftward)
    return spread + spread.T


def body(
    diag_two,
    diag_one,
    cross_tile,
    left_two,
    left_one,
    below_left,
    panel_two,
    panel_one,
    grad_diag_two,
    grad_diag_one,
    grad_cross,
    grad_left_two,
    grad_left_one,
    grad_below,
    grad_panel_two,
    grad_panel_one,
):
    share = grad_left_two.shape[0]
    width = panel_two.shape[1]
    row_start = lax.axis_index("row") * share
    col_start = lax.axis_index("col") * width
    grad_two_all, panel_two_all, grad_one_all, panel_one_all = gather_turned(
        (grad_panel_two, panel_two, grad_panel_one, panel_one), "col", (1, 1, 1, 1)
    )
    solved_two = right_solve(diag_two, grad_two_all)
    gram_two, gram_cross = (
        gathered_total(matmul(solved_two.T, panel_two_all), "row"),
        gathered_total(matmul(solved_two.T, panel_one_all), "row"),
    )
    below_first = grad_below - matmul(solved_two, left_two)
    sym_two = reverse_block(diag_two, grad_diag_two - jnp.tril(gram_two))
    cross_next = grad_cross - gram_cross - matmul(sym_two, cross_tile)
    out_cross = right_solve(diag_one, cross_next)
    panel_next = grad_one_all - matmul(solved_two, cross_tile)
    out_panel_one = right_solve(diag_one, panel_next)
    gram_below = taken_together(matmul(out_panel_one.T, panel_one_all), "row")
    summed_both = sum_at_owner(
        jnp.concatenate(
            [matmul(solved_two.T, below_left), matmul(out_panel_one.T, below_left)], axis=1
        ),
        "row",
        0,
    )
    summed_two = summed_both[:, : left_two.shape[1]]
    summed_one = summed_both[:, left_two.shape[1] :]
    out_below = below_first - matmul(out_panel_one, left_one)
    gram_one = matmul(out_cross.T, cross_tile) + gram_below
    sym_one = reverse_block(diag_one, grad_diag_one - jnp.tril(gram_one))
    sym_two_rows = lax.dynamic_slice_in_dim(sym_two, row_start, share, 0)
    sym_one_rows = lax.dynamic_slice_in_dim(sym_one, row_start, share, 0)
    cross_rows = lax.dynamic_slice_in_dim(out_cross, row_start, share, 0)
    cross_cols = lax.dynamic_slice_in_dim(out_cross, row_start, share, 1)
    out_left_two = (
        grad_left_two - summed_two - matmul(sym_two_rows, left_two) - matmul(cross_rows, left_one)
    )
    out_left_one = (
        grad_left_one - matmul(cross_cols.T, left_two) - summed_one - matmul(sym_one_rows, left_one)
    )
    out_panel_two = lax.dynamic_slice_in_dim(solved_two, col_start, width, 1)
    panel_one_cols = lax.dynamic_slice_in_dim(out_panel_one, col_start, width, 1)
    return (
        out_below,
        out_left_two,
        out_left_one,
        halved(sym_two),
        halved(sym_one),
        out_cross,
        out_panel_two,
        panel_one_cols,
    )


def solution(mesh):
    return jax.shard_map(
        body,
        mesh=mesh,
        in_specs=(
            P(),
            P(),
            P(),
            P(None, ("col", "depth")),
            P(None, ("col", "depth")),
            P("row", ("col", "depth")),
            P("row", "col"),
            P("row", "col"),
            P(),
            P(),
            P(),
            P("row", ("col", "depth")),
            P("row", ("col", "depth")),
            P("row", ("col", "depth")),
            P("row", "col"),
            P("row", "col"),
        ),
        out_specs=(
            P("row", ("col", "depth")),
            P("row", ("col", "depth")),
            P("row", ("col", "depth")),
            P(),
            P(),
            P(),
            P("row", "col"),
            P("row", "col"),
        ),
        check_vma=False,
    )
```

profile of v0, /device:TPU:1, one launch (start us, length us, event | category | flops | bytes accessed | tf_op | source)
XLA Modules:
  0.0 182.9 jit_solution(14696959862518335248)
XLA Ops:
  10.2 4.0 %while.14 = (s32[]{:T(128)}, f32[256,256]{1,0:T(8,128)S(1)}, s32[2,2]{1,0:T(2,128)S(1)}, f32[2,128,128]{2,1,0:T(8,128)S(1)}, s32[]{:T(128)}) while((s32[]{:T(128)}, f32[256,256]{1,0:T(8,128)S(1)}, s32[2,2]{1,0:T(2,128)S(1)}, f32[2,128,128]{2,1,0:T(8,128)S(1)}, s32[]{:T(128)}) %tuple.63), condition=%wide.while_cond, body=%wide.while_body.sunk | while | flops 2 | bytes 131181 | solution.py:50
  14.2 20.3 %custom-call.21 = f32[2,128,128]{1,2,0:T(8,128)} custom-call(f32[2,128,128]{2,1,0:T(8,128)S(1)} %get-tuple-element.59), custom_call_target="InvertDiagBlocksLowerTriangular" | custom-call | tf_op jit(solution)/shard_map/triangular_solve/custom-call.1 | solution.py:50
  35.4 4.0 %while.15 = (s32[]{:T(128)}, f32[256,256]{1,0:T(8,128)S(1)}, s32[2,2]{1,0:T(2,128)S(1)}, f32[2,128,128]{2,1,0:T(8,128)S(1)}, s32[]{:T(128)}) while((s32[]{:T(128)}, f32[256,256]{1,0:T(8,128)S(1)}, s32[2,2]{1,0:T(2,128)S(1)}, f32[2,128,128]{2,1,0:T(8,128)S(1)}, s32[]{:T(128)}) %tuple.75), condition=%wide.while_cond.clone, body=%wide.while_body.clone.sunk | while | flops 2 | bytes 131181 | solution.py:50
  39.4 19.9 %custom-call.22 = f32[2,128,128]{1,2,0:T(8,128)S(1)} custom-call(f32[2,128,128]{2,1,0:T(8,128)S(1)} %get-tuple-element.60), custom_call_target="InvertDiagBlocksLowerTriangular" | custom-call | tf_op jit(solution)/shard_map/triangular_solve/custom-call.1 | solution.py:50
  60.2 11.3 %all-gather.6.cloned.1.call-done = f32[256,4096]{1,0:T(8,128)} async-done(((f32[16,4096]{1,0:T(8,128)}), f32[256,4096]{1,0:T(8,128)}) %all-gather.6.cloned.1.call-update) | async-done | bytes 4194320 | tf_op jit(solution)/shard_map/all_gather | solution.py:10
  71.5 2.7 %fusion.74 = (f32[256,1024]{1,0:T(8,128)}, f32[256,1024]{1,0:T(8,128)S(1)}) fusion(f32[256,4096]{1,0:T(8,128)} %all-gather.6.cloned.1.call-done), kind=kLoop, calls=%fused_computation.134 | loop fusion | bytes 4194304 | tf_op jit(solution)/shard_map/slice | solution.py:12
  80.0 3.0 %fusion.3 = f32[256,256]{1,0:T(8,128)} fusion(f32[256,4096]{1,0:T(8,128)} %all-gather.6.cloned.1.call-done, f32[1024,128]{0,1:T(8,128)S(1)} %bitcast.124, f32[1024,128]{0,1:T(8,128)S(1)} %fusion.43), kind=kOutput, calls=%fused_computation.34 | convolution fusion | flops 805568512 | bytes 2359296 | tf_op jit(solution)/shard_map/dot_general | solution.py:46
  83.0 2.5 %copy.95 = f32[256,1024]{0,1:T(8,128)} copy(f32[256,1024]{1,0:T(8,128)} %get-tuple-element.118) | data formatting | bytes 2097152
  85.6 3.2 %convolution_subtract_fusion = f32[1024,256]{1,0:T(8,128)S(1)} fusion(f32[256,256]{1,0:T(8,128)} %param.24, f32[256,1024]{0,1:T(8,128)} %copy.95, f32[1024,128]{0,1:T(8,128)S(1)} %bitcast.125, f32[1024,128]{0,1:T(8,128)S(1)} %fusion.43), kind=kOutput, calls=%fused_computation.9 | convolution fusion | flops 805830656 | bytes 3407872 | tf_op jit(solution)/shard_map/dot_general | solution.py:46
  91.8 2.3 %fusion.5 = f32[256,256]{1,0:T(8,128)S(1)} fusion(f32[256,4096]{1,0:T(8,128)} %all-gather.6.cloned.1.call-done, f32[1024,128]{0,1:T(8,128)S(1)} %bitcast.130, f32[1024,128]{0,1:T(8,128)S(1)} %fusion.50), kind=kOutput, calls=%fused_computation.37 | convolution fusion | flops 805568512 | bytes 2359296 | tf_op jit(solution)/shard_map/dot_general | solution.py:46
  95.2 5.0 %all-to-all-start.1 = ((f32[4,256,256]{2,1,0:T(8,128)}), f32[4,256,256]{2,1,0:T(8,128)}, u32[]{:S(2)}, u32[]{:S(2)}) async-start(f32[4,256,256]{2,1,0:T(8,128)} %broadcast_in_dim.66), calls=%async_computation.1 | async-start | bytes 2097152 | tf_op jit(solution)/shard_map/all_to_all | solution.py:25
  102.3 3.0 %fusion.7 = f32[256,256]{1,0:T(8,128)} fusion(f32[256,4096]{1,0:T(8,128)} %all-gather.6.cloned.1.call-done, f32[1024,128]{0,1:T(8,128)S(1)} %bitcast.127, f32[1024,128]{0,1:T(8,128)S(1)} %fusion.43), kind=kOutput, calls=%fused_computation.39 | convolution fusion | flops 805568512 | bytes 2359296 | tf_op jit(solution)/shard_map/dot_general | solution.py:46
  105.3 3.9 %fusion.9 = f32[256,512]{1,0:T(8,128)} fusion(f32[1024,512]{1,0:T(8,128)S(1)} %copy-done, f32[1024,128]{0,1:T(8,128)} %bitcast.132, f32[1024,128]{0,1:T(8,128)} %copy-done.3), kind=kOutput, calls=%fused_computation.41 | convolution fusion | flops 1610874880 | bytes 3670016 | tf_op jit(solution)/shard_map/dot_general | solution.py:46
  109.3 2.7 %fusion.14 = f32[256,512]{1,0:T(8,128)} fusion(f32[1024,512]{1,0:T(8,128)S(1)} %copy-done, f32[1024,128]{0,1:T(8,128)S(1)} %bitcast.128, f32[1024,128]{0,1:T(8,128)S(1)} %fusion.43), kind=kOutput, calls=%fused_computation.51 | convolution fusion | flops 1610874880 | bytes 3670016 | tf_op jit(solution)/shard_map/dot_general | solution.py:46
  112.0 3.2 %fusion.15 = f32[1024,512]{1,0:T(8,128)} fusion(f32[256,512]{1,0:T(8,128)S(1)} %copy-done.5, f32[1024,128]{0,1:T(8,128)S(1)} %bitcast.129, f32[1024,128]{0,1:T(8,128)S(1)} %fusion.43), kind=kOutput, calls=%fused_computation.52 | convolution fusion | flops 1610874880 | bytes 3670016 | tf_op jit(solution)/shard_map/dot_general | solution.py:46
  115.2 2.4 %pad_maximum_fusion.2 = f32[256,1024]{1,0:T(8,128)} fusion(f32[256,512]{1,0:T(8,128)} %fusion.9, f32[256,512]{1,0:T(8,128)} %fusion.14), kind=kLoop, calls=%fused_computation.36 | loop fusion | flops 262144 | bytes 2097152 | tf_op jit(solution)/shard_map/concatenate | solution.py:104
  117.6 5.5 %subtract_subtract_fusion = f32[1024,512]{1,0:T(8,128)} fusion(f32[1024,512]{1,0:T(8,128)} %param.35, f32[1024,512]{1,0:T(8,128)} %fusion.15, f32[256,512]{1,0:T(8,128)S(1)} %copy-done.7, f32[1024,128]{0,1:T(8,128)S(1)} %bitcast.133, f32[1024,128]{0,1:T(8,128)S(1)} %copy-done.4), kind=kOutput, calls=%fused_computation.8 | convolution fusion | flops 1611923456 | bytes 7864320 | tf_op jit(solution)/shard_map/dot_general | solution.py:46
  126.1 2.6 %gather_fusion = f32[256]{0:T(256)S(1)} fusion(f32[256,256]{0,1:T(8,128)S(1)} %convolution_bitcast_fusion.1, s32[256]{0:T(256)S(1)} %bitcast.120), kind=kCustom, calls=%fused_computation | custom fusion | bytes 4096 | tf_op jit(solution)/shard_map/jit(_diag)/jit(diagonal)/cond/branch_0_fun/gather | solution.py:54
  131.7 6.9 %all-gather.10.cloned.1.call-done = f32[1024,256]{1,0:T(8,128)} async-done(((f32[256,256]{1,0:T(8,128)}), f32[1024,256]{1,0:T(8,128)}) %all-gather.10.cloned.1.call-update) | async-done | bytes 1048592 | tf_op jit(solution)/shard_map/all_gather | solution.py:19
  144.2 4.4 %all-to-all-start = ((f32[4,64,1024]{2,1,0:T(8,128)}), f32[4,64,1024]{2,1,0:T(8,128)}, u32[]{:S(2)}, u32[]{:S(2)}) async-start(f32[4,64,1024]{2,1,0:T(8,128)} %bitcast.140), calls=%async_computation | async-start | bytes 2097152 | tf_op jit(solution)/shard_map/all_to_all | solution.py:41
  153.8 2.4 %gather_fusion.1 = f32[256]{0:T(256)S(1)} fusion(f32[256,256]{0,1:T(8,128)S(1)} %convolution_bitcast_fusion, s32[256]{0:T(256)S(1)} %bitcast.121), kind=kCustom, calls=%fused_computation.1 | custom fusion | bytes 4096 | tf_op jit(solution)/shard_map/jit(_diag)/jit(diagonal)/cond/branch_0_fun/gather | solution.py:54
  157.2 2.4 %gather_fusion.2 = f32[256]{0:T(256)S(1)} fusion(f32[256,256]{0,1:T(8,128)S(1)} %bitcast_add_fusion.1, s32[256]{0:T(256)S(1)} %bitcast.122), kind=kCustom, calls=%fused_computation.2 | custom fusion | bytes 4096 | tf_op jit(solution)/shard_map/jit(_diag)/jit(diagonal)/cond/branch_0_fun/gather | solution.py:54
  161.7 2.4 %gather_fusion.3 = f32[256]{0:T(256)S(1)} fusion(f32[256,256]{0,1:T(8,128)S(1)} %bitcast_add_fusion, s32[256]{0:T(256)S(1)} %bitcast.123), kind=kCustom, calls=%fused_computation.3 | custom fusion | bytes 4096 | tf_op jit(solution)/shard_map/jit(_diag)/jit(diagonal)/cond/branch_0_fun/gather | solution.py:54
  172.6 2.2 %convolution_subtract_fusion.4 = f32[64,512]{1,0:T(8,128)} fusion(f32[64,512]{1,0:T(8,128)S(1)} %fusion.2, f32[256,512]{1,0:T(8,128)} %param.26, f32[256,256]{0,1:T(8,128)S(1)} %bitcast_add_fusion, s32[]{:T(128)S(6)} %select_n.58), kind=kOutput, calls=%fused_computation.24 | convolution fusion | flops 100696064 | bytes 917508 | tf_op jit(solution)/shard_map/dot_general | solution.py:46
  (137 shorter events, 54.2 us)
Async XLA Ops:
  7.2 98.2 %copy-start = (f32[1024,512]{1,0:T(8,128)S(1)}, f32[1024,512]{1,0:T(8,128)}, u32[]{:S(2)}) copy-start(f32[1024,512]{1,0:T(8,128)} %param.27) | copy-start | bytes 6291460
  7.2 27.4 %copy-start.22 = (f32[256,256]{1,0:T(8,128)S(1)}, f32[256,256]{1,0:T(8,128)}, u32[]{:S(2)}) copy-start(f32[256,256]{1,0:T(8,128)} %param.30) | copy-start | bytes 786436
  7.2 28.2 %copy-start.19 = (f32[256,256]{1,0:T(8,128)S(1)}, f32[256,256]{1,0:T(8,128)}, u32[]{:S(2)}) copy-start(f32[256,256]{1,0:T(8,128)} %param.23) | copy-start | bytes 786436
  7.2 64.3 %all-gather.6.cloned.1.call-start = ((), (), s32[]{:S(2)}) async-start(), calls=%async_computation.2 | async-start | bytes 4456448 | tf_op jit(solution)/shard_map/all_gather | solution.py:10
  7.3 52.1 %copy-start.23 = (f32[256,256]{1,0:T(8,128)S(1)}, f32[256,256]{1,0:T(8,128)}, u32[]{:S(2)}) copy-start(f32[256,256]{1,0:T(8,128)} %param.31) | copy-start | bytes 786436
  9.1 114.0 %all-gather.8.cloned.1.call-start = ((), (), s32[]{:S(2)}) async-start(), calls=%async_computation.3 | async-start | bytes 1310720 | tf_op jit(solution)/shard_map/all_gather | solution.py:19
  14.2 46.0 %copy-start.11 = (f32[256,256]{1,0:T(8,128)}, f32[256,256]{1,0:T(8,128)S(1)}, u32[]{:S(2)}) copy-start(f32[256,256]{1,0:T(8,128)S(1)} %get-tuple-element.217) | copy-start | bytes 786436
  39.4 104.1 %copy-start.9 = (f32[256,256]{1,0:T(8,128)}, f32[256,256]{1,0:T(8,128)S(1)}, u32[]{:S(2)}) copy-start(f32[256,256]{1,0:T(8,128)S(1)} %get-tuple-element.216) | copy-start | bytes 786436
  59.3 31.1 %copy-start.14 = (f32[2,128,128]{1,2,0:T(8,128)}, f32[2,128,128]{1,2,0:T(8,128)S(1)}, u32[]{:S(2)}) copy-start(f32[2,128,128]{1,2,0:T(8,128)S(1)} %custom-call.22) | copy-start | bytes 393220
  75.6 3.8 %copy-start.17 = (f32[2,128,128]{1,2,0:T(8,128)S(1)}, f32[2,128,128]{1,2,0:T(8,128)}, u32[]{:S(2)}) copy-start(f32[2,128,128]{1,2,0:T(8,128)} %custom-call.21) | copy-start | bytes 393220
  89.4 4.8 %copy-start.1 = (f32[128,1024]{1,0:T(8,128)}, f32[128,1024]{1,0:T(8,128)S(1)}, u32[]{:S(2)}) copy-start(f32[128,1024]{1,0:T(8,128)S(1)} %fusion.10) | copy-start | bytes 1572868
  95.2 49.0 %all-to-all-start.1 = ((f32[4,256,256]{2,1,0:T(8,128)}), f32[4,256,256]{2,1,0:T(8,128)}, u32[]{:S(2)}, u32[]{:S(2)}) async-start(f32[4,256,256]{2,1,0:T(8,128)} %broadcast_in_dim.66), calls=%async_computation.1 | async-start | bytes 2097152 | tf_op jit(solution)/shard_map/all_to_all | solution.py:25
  100.2 38.3 %all-gather.10.cloned.1.call-start = ((), (), s32[]{:S(2)}) async-start(), calls=%async_computation.4 | async-start | bytes 1310720 | tf_op jit(solution)/shard_map/all_gather | solution.py:19
  123.1 5.6 %copy-start.18 = (f32[2,128,128]{1,2,0:T(8,128)S(1)}, f32[2,128,128]{1,2,0:T(8,128)}, u32[]{:S(2)}) copy-start(f32[2,128,128]{1,2,0:T(8,128)} %custom-call.21) | copy-start | bytes 393220
  124.5 4.6 %copy-start.12 = (f32[256,256]{1,0:T(8,128)S(1)}, f32[256,256]{1,0:T(8,128)}, u32[]{:S(2)}) copy-start(f32[256,256]{1,0:T(8,128)} %copy-done.11) | copy-start | bytes 786436
  130.0 11.5 %copy-start.13 = (f32[256,256]{1,0:T(8,128)S(1)}, f32[256,256]{1,0:T(8,128)}, u32[]{:S(2)}) copy-start(f32[256,256]{1,0:T(8,128)} %param.24) | copy-start | bytes 786436
  130.8 12.4 %copy-start.15 = (f32[2,128,128]{1,2,0:T(8,128)S(1)}, f32[2,128,128]{1,2,0:T(8,128)}, u32[]{:S(2)}) copy-start(f32[2,128,128]{1,2,0:T(8,128)} %copy-done.14) | copy-start | bytes 393220
  144.2 6.6 %copy-start.20 = (f32[256,256]{0,1:T(8,128)S(1)}, f32[256,256]{0,1:T(8,128)}, u32[]{:S(2)}) copy-start(f32[256,256]{0,1:T(8,128)} %copy.81) | copy-start | bytes 786436
  144.2 24.9 %all-to-all-start = ((f32[4,64,1024]{2,1,0:T(8,128)}), f32[4,64,1024]{2,1,0:T(8,128)}, u32[]{:S(2)}, u32[]{:S(2)}) async-start(f32[4,64,1024]{2,1,0:T(8,128)} %bitcast.140), calls=%async_computation | async-start | bytes 2097152 | tf_op jit(solution)/shard_map/all_to_all | solution.py:41
  150.0 6.2 %copy-start.16 = (f32[2,128,128]{1,2,0:T(8,128)S(1)}, f32[2,128,128]{1,2,0:T(8,128)}, u32[]{:S(2)}) copy-start(f32[2,128,128]{1,2,0:T(8,128)} %copy-done.14) | copy-start | bytes 393220
  150.8 5.7 %copy-start.10 = (f32[256,256]{1,0:T(8,128)S(1)}, f32[256,256]{1,0:T(8,128)}, u32[]{:S(2)}) copy-start(f32[256,256]{1,0:T(8,128)} %copy-done.9) | copy-start | bytes 786436
  161.7 9.5 %copy-start.6 = (f32[256,512]{1,0:T(8,128)S(1)}, f32[256,512]{1,0:T(8,128)}, u32[]{:S(2)}) copy-start(f32[256,512]{1,0:T(8,128)} %param.25) | copy-start | bytes 1572868
  161.7 9.5 %copy-start.24 = (f32[64,512]{1,0:T(8,128)S(1)}, f32[64,512]{1,0:T(8,128)}, u32[]{:S(2)}) copy-start(f32[64,512]{1,0:T(8,128)} %param.34) | copy-start | bytes 393220
  171.1 4.1 %copy-start.8 = (f32[256,512]{1,0:T(8,128)S(1)}, f32[256,512]{1,0:T(8,128)}, u32[]{:S(2)}) copy-start(f32[256,512]{1,0:T(8,128)} %param.26) | copy-start | bytes 1572868
  (7 other events, 18.1 us)
Sparse Core Ops, SparseCore 0:
  11.0 60.4 all-gather.5
  83.1 27.1 all-gather.7
  115.3 23.1 all-gather.9
where the time goes:
time: 184 us; the launch traced here: 183 us
  other arithmetic  56.8 us (31%)
  matrix products  49.2 us (27%)
  local copies, waits for them, and re-layouts  34.6 us (19%)
  waiting for transfers between devices  18.3 us (10%)
  between operations  14.4 us (8%)
  starting transfers between devices  9.55 us (5%)
    another operation x10, other arithmetic, right_solve(): lax.linalg.triangular_solve(factor, values, left_side=False, lower=True)  43.3 us
    dot_general x16, matrix products, matmul(): jnp.dot(left, right, precision=lax.Precision.HIGHEST, preferred_element_t...  37.9 us
    all_gather x1, waiting for transfers between devices, gather_turned(): out, at, outs = (lax.all_gather(both, axis, axis=0, tiled=True), 0, [])  11.3 us
    unnamed x59, local copies, waits for them, and re-layouts  11 us
    gather x4, local copies, waits for them, and re-layouts, halved(): return jnp.tril(square) - 0.5 * jnp.diag(jnp.diag(square))  9.74 us
    another operation x15, matrix products, right_solve(): lax.linalg.triangular_solve(factor, values, left_side=False, lower=True)  9.4 us
    another operation x19, local copies, waits for them, and re-layouts, right_solve(): lax.linalg.triangular_solve(factor, values, left_side=False, lower=True)  9.14 us
    all_gather x2, waiting for transfers between devices, gathered_total(): blocks = lax.all_gather(value, axis)  6.87 us
  transfers between devices with their start and end apart: 5, of which 2 were waited for; matrix products, arithmetic and copies ran while one was open for 65% of the time, Pallas kernels for 0%

commit v1 on v0

--- a/solution.py
+++ b/solution.py
@@ -7,7 +7,13 @@
 def gather_turned(arrays, axis, dims):
     turned = [jnp.moveaxis(a, dim, 0) for a, dim in zip(arrays, dims)]
     both = jnp.concatenate([t.reshape(len(t), -1) for t in turned], axis=1)
-    out, at, outs = (lax.all_gather(both, axis, axis=0, tiled=True), 0, [])
+    out, at, outs = (
+        jnp.concatenate(
+            lax.all_to_all(jnp.stack([both] * lax.axis_size(axis)), axis, 0, 0), axis=0
+        ),
+        0,
+        [],
+    )
     for t, dim in zip(turned, dims):
         piece = out[:, at : at + t[0].size].reshape(-1, *t.shape[1:])
         outs.append(jnp.moveaxis(piece, 0, dim))

time: 184 us -> 198 us (1.076)
  starting transfers between devices: 9.55 us -> 18.4 us
  local copies, waits for them, and re-layouts: 34.6 us -> 38.1 us
  waiting for transfers between devices: 18.3 us -> 20.9 us
    all_gather x1 -> x0, waiting for transfers between devices: 11.3 us -> none  [gather_turned(): out, at, outs = (lax.all_gather(both, axis, axis=0, tiled=True), 0, [])]
    all_to_all x0 -> x1, waiting for transfers between devices: none -> 11.2 us  [gather_turned(): lax.all_to_all(jnp.stack([both] * lax.axis_size(axis)), axis, 0, 0)]
    all_to_all x0 -> x1, starting transfers between devices: none -> 7.77 us  [gather_turned(): lax.all_to_all(jnp.stack([both] * lax.axis_size(axis)), axis, 0, 0)]
    all_gather x2, waiting for transfers between devices: 6.87 us -> 9.67 us  [gathered_total(): blocks = lax.all_gather(value, axis)]
    another operation x0 -> x1, local copies, waits for them, and re-layouts: none -> 2.49 us  [gather_turned(): jnp.stack([both] * lax.axis_size(axis))]
  transfers between devices with their start and end apart: 5 -> 5, of which waited for: 2 -> 2; matrix products, arithmetic and copies ran while one was open for 65% -> 61% of each run, Pallas kernels for 0% -> 0%
where the time goes in v1:
time: 198 us; the launch traced here: 197 us
  other arithmetic  55.2 us (28%)
  matrix products  49.2 us (25%)
  local copies, waits for them, and re-layouts  38.1 us (19%)
  waiting for transfers between devices  20.9 us (11%)
  starting transfers between devices  18.4 us (9%)
  between operations  14.7 us (7%)
    another operation x10, other arithmetic, right_solve(): lax.linalg.triangular_solve(factor, values, left_side=False, lower=True)  42.4 us
    dot_general x16, matrix products, matmul(): jnp.dot(left, right, precision=lax.Precision.HIGHEST, preferred_element_t...  37.9 us
    unnamed x59, local copies, waits for them, and re-layouts  12 us
    all_to_all x1, waiting for transfers between devices, gather_turned(): lax.all_to_all(jnp.stack([both] * lax.axis_size(axis)), axis, 0, 0)  11.2 us
    gather x4, local copies, waits for them, and re-layouts, halved(): return jnp.tril(square) - 0.5 * jnp.diag(jnp.diag(square))  9.74 us
    all_gather x2, waiting for transfers between devices, gathered_total(): blocks = lax.all_gather(value, axis)  9.67 us
    another operation x15, matrix products, right_solve(): lax.linalg.triangular_solve(factor, values, left_side=False, lower=True)  9.39 us
    another operation x19, local copies, waits for them, and re-layouts, right_solve(): lax.linalg.triangular_solve(factor, values, left_side=False, lower=True)  9.13 us
  transfers between devices with their start and end apart: 5, of which 2 were waited for; matrix products, arithmetic and copies ran while one was open for 61% of the time, Pallas kernels for 0%

profile of v1, /device:TPU:1, one launch (start us, length us, event | category | flops | bytes accessed | tf_op | source)
XLA Modules:
  0.0 196.5 jit_solution(3735488551449046491)
XLA Ops:
  8.3 2.5 %stack.2 = f32[16,16,4096]{2,1,0:T(8,128)} broadcast(f32[16,4096]{1,0:T(8,128)S(1)} %pad_maximum_fusion.12), dimensions={1,2} | broadcast | bytes 4456448 | tf_op jit(solution)/shard_map/stack | solution.py:12
  10.8 7.8 %all-to-all-start = ((f32[16,16,4096]{2,1,0:T(8,128)}), f32[16,16,4096]{2,1,0:T(8,128)}, u32[]{:S(2)}, u32[]{:S(2)}) async-start(f32[16,16,4096]{2,1,0:T(8,128)} %stack.2), calls=%async_computation | async-start | bytes 8388608 | tf_op jit(solution)/shard_map/all_to_all | solution.py:12
  18.8 4.0 %while.14 = (s32[]{:T(128)}, f32[256,256]{1,0:T(8,128)S(1)}, s32[2,2]{1,0:T(2,128)S(1)}, f32[2,128,128]{2,1,0:T(8,128)S(1)}, s32[]{:T(128)}) while((s32[]{:T(128)}, f32[256,256]{1,0:T(8,128)S(1)}, s32[2,2]{1,0:T(2,128)S(1)}, f32[2,128,128]{2,1,0:T(8,128)S(1)}, s32[]{:T(128)}) %tuple.63), condition=%wide.while_cond, body=%wide.while_body.sunk | while | flops 2 | bytes 131181 | solution.py:56
  22.8 20.3 %custom-call.21 = f32[2,128,128]{1,2,0:T(8,128)} custom-call(f32[2,128,128]{2,1,0:T(8,128)S(1)} %get-tuple-element.59), custom_call_target="InvertDiagBlocksLowerTriangular" | custom-call | tf_op jit(solution)/shard_map/triangular_solve/custom-call.1 | solution.py:56
  44.0 4.0 %while.15 = (s32[]{:T(128)}, f32[256,256]{1,0:T(8,128)S(1)}, s32[2,2]{1,0:T(2,128)S(1)}, f32[2,128,128]{2,1,0:T(8,128)S(1)}, s32[]{:T(128)}) while((s32[]{:T(128)}, f32[256,256]{1,0:T(8,128)S(1)}, s32[2,2]{1,0:T(2,128)S(1)}, f32[2,128,128]{2,1,0:T(8,128)S(1)}, s32[]{:T(128)}) %tuple.73), condition=%wide.while_cond.clone, body=%wide.while_body.clone.sunk | while | flops 2 | bytes 131181 | solution.py:56
  48.0 19.9 %custom-call.22 = f32[2,128,128]{1,2,0:T(8,128)S(1)} custom-call(f32[2,128,128]{2,1,0:T(8,128)S(1)} %get-tuple-element.60), custom_call_target="InvertDiagBlocksLowerTriangular" | custom-call | tf_op jit(solution)/shard_map/triangular_solve/custom-call.1 | solution.py:56
  69.7 11.2 %all-to-all-done = f32[16,16,4096]{2,1,0:T(8,128)} async-done(((f32[16,16,4096]{2,1,0:T(8,128)}), f32[16,16,4096]{2,1,0:T(8,128)}, u32[]{:S(2)}, u32[]{:S(2)}) %all-to-all-start) | async-done | bytes 4194336 | tf_op jit(solution)/shard_map/all_to_all | solution.py:12
  80.9 2.7 %fusion.74 = (f32[256,1024]{1,0:T(8,128)}, f32[256,1024]{1,0:T(8,128)S(1)}) fusion(f32[256,4096]{1,0:T(8,128)} %bitcast.4), kind=kLoop, calls=%fused_computation.134 | loop fusion | bytes 4194304 | tf_op jit(solution)/shard_map/slice | solution.py:18
  89.4 3.0 %fusion.3 = f32[256,256]{1,0:T(8,128)} fusion(f32[256,4096]{1,0:T(8,128)} %bitcast.4, f32[1024,128]{0,1:T(8,128)S(1)} %bitcast.125, f32[1024,128]{0,1:T(8,128)S(1)} %fusion.43), kind=kOutput, calls=%fused_computation.34 | convolution fusion | flops 805568512 | bytes 2359296 | tf_op jit(solution)/shard_map/dot_general | solution.py:52
  92.4 2.6 %copy.89 = f32[256,1024]{0,1:T(8,128)} copy(f32[256,1024]{1,0:T(8,128)} %get-tuple-element.118) | data formatting | bytes 2097152
  94.9 3.2 %convolution_subtract_fusion = f32[1024,256]{1,0:T(8,128)S(1)} fusion(f32[256,256]{1,0:T(8,128)} %param.24, f32[256,1024]{0,1:T(8,128)} %copy.89, f32[1024,128]{0,1:T(8,128)S(1)} %bitcast.126, f32[1024,128]{0,1:T(8,128)S(1)} %fusion.43), kind=kOutput, calls=%fused_computation.9 | convolution fusion | flops 805830656 | bytes 3407872 | tf_op jit(solution)/shard_map/dot_general | solution.py:52
  104.6 6.0 %all-to-all-start.2 = ((f32[4,256,256]{2,1,0:T(8,128)}), f32[4,256,256]{2,1,0:T(8,128)}, u32[]{:S(2)}, u32[]{:S(2)}) async-start(f32[4,256,256]{2,1,0:T(8,128)} %broadcast_in_dim.66), calls=%async_computation.2 | async-start | bytes 2097152 | tf_op jit(solution)/shard_map/all_to_all | solution.py:31
  112.7 3.0 %fusion.7 = f32[256,256]{1,0:T(8,128)} fusion(f32[256,4096]{1,0:T(8,128)} %bitcast.4, f32[1024,128]{0,1:T(8,128)S(1)} %bitcast.128, f32[1024,128]{0,1:T(8,128)S(1)} %fusion.43), kind=kOutput, calls=%fused_computation.39 | convolution fusion | flops 805568512 | bytes 2359296 | tf_op jit(solution)/shard_map/dot_general | solution.py:52
  115.7 3.9 %fusion.9 = f32[256,512]{1,0:T(8,128)} fusion(f32[1024,512]{1,0:T(8,128)S(1)} %copy-done, f32[1024,128]{0,1:T(8,128)} %bitcast.133, f32[1024,128]{0,1:T(8,128)} %copy-done.3), kind=kOutput, calls=%fused_computation.41 | convolution fusion | flops 1610874880 | bytes 3670016 | tf_op jit(solution)/shard_map/dot_general | solution.py:52
  119.6 2.7 %fusion.14 = f32[256,512]{1,0:T(8,128)} fusion(f32[1024,512]{1,0:T(8,128)S(1)} %copy-done, f32[1024,128]{0,1:T(8,128)S(1)} %bitcast.129, f32[1024,128]{0,1:T(8,128)S(1)} %fusion.43), kind=kOutput, calls=%fused_computation.51 | convolution fusion | flops 1610874880 | bytes 3670016 | tf_op jit(solution)/shard_map/dot_general | solution.py:52
  122.4 3.2 %fusion.15 = f32[1024,512]{1,0:T(8,128)} fusion(f32[256,512]{1,0:T(8,128)S(1)} %copy-done.5, f32[1024,128]{0,1:T(8,128)S(1)} %bitcast.130, f32[1024,128]{0,1:T(8,128)S(1)} %fusion.43), kind=kOutput, calls=%fused_computation.52 | convolution fusion | flops 1610874880 | bytes 3670016 | tf_op jit(solution)/shard_map/dot_general | solution.py:52
  125.6 2.4 %pad_maximum_fusion.2 = f32[256,1024]{1,0:T(8,128)} fusion(f32[256,512]{1,0:T(8,128)} %fusion.9, f32[256,512]{1,0:T(8,128)} %fusion.14), kind=kLoop, calls=%fused_computation.36 | loop fusion | flops 262144 | bytes 2097152 | tf_op jit(solution)/shard_map/concatenate | solution.py:110
  128.0 5.5 %subtract_subtract_fusion = f32[1024,512]{1,0:T(8,128)} fusion(f32[1024,512]{1,0:T(8,128)} %param.35, f32[1024,512]{1,0:T(8,128)} %fusion.15, f32[256,512]{1,0:T(8,128)S(1)} %copy-done.7, f32[1024,128]{0,1:T(8,128)S(1)} %bitcast.134, f32[1024,128]{0,1:T(8,128)S(1)} %copy-done.4), kind=kOutput, calls=%fused_computation.8 | convolution fusion | flops 1611923456 | bytes 7864320 | tf_op jit(solution)/shard_map/dot_general | solution.py:52
  136.5 2.6 %gather_fusion = f32[256]{0:T(256)S(1)} fusion(f32[256,256]{0,1:T(8,128)S(1)} %convolution_bitcast_fusion.1, s32[256]{0:T(256)S(1)} %bitcast.121), kind=kCustom, calls=%fused_computation | custom fusion | bytes 4096 | tf_op jit(solution)/shard_map/jit(_diag)/jit(diagonal)/cond/branch_0_fun/gather | solution.py:60
  142.1 9.7 %all-gather.7.cloned.1.call-done = f32[1024,256]{1,0:T(8,128)} async-done(((f32[256,256]{1,0:T(8,128)}), f32[1024,256]{1,0:T(8,128)}) %all-gather.7.cloned.1.call-update) | async-done | bytes 1048592 | tf_op jit(solution)/shard_map/all_gather | solution.py:25
  157.4 4.6 %all-to-all-start.1 = ((f32[4,64,1024]{2,1,0:T(8,128)}), f32[4,64,1024]{2,1,0:T(8,128)}, u32[]{:S(2)}, u32[]{:S(2)}) async-start(f32[4,64,1024]{2,1,0:T(8,128)} %bitcast.141), calls=%async_computation.1 | async-start | bytes 2097152 | tf_op jit(solution)/shard_map/all_to_all | solution.py:47
  167.1 2.4 %gather_fusion.1 = f32[256]{0:T(256)S(1)} fusion(f32[256,256]{0,1:T(8,128)S(1)} %convolution_bitcast_fusion, s32[256]{0:T(256)S(1)} %bitcast.122), kind=kCustom, calls=%fused_computation.1 | custom fusion | bytes 4096 | tf_op jit(solution)/shard_map/jit(_diag)/jit(diagonal)/cond/branch_0_fun/gather | solution.py:60
  170.5 2.4 %gather_fusion.2 = f32[256]{0:T(256)S(1)} fusion(f32[256,256]{0,1:T(8,128)S(1)} %bitcast_add_fusion.1, s32[256]{0:T(256)S(1)} %bitcast.123), kind=kCustom, calls=%fused_computation.2 | custom fusion | bytes 4096 | tf_op jit(solution)/shard_map/jit(_diag)/jit(diagonal)/cond/branch_0_fun/gather | solution.py:60
  175.0 2.4 %gather_fusion.3 = f32[256]{0:T(256)S(1)} fusion(f32[256,256]{0,1:T(8,128)S(1)} %bitcast_add_fusion, s32[256]{0:T(256)S(1)} %bitcast.124), kind=kCustom, calls=%fused_computation.3 | custom fusion | bytes 4096 | tf_op jit(solution)/shard_map/jit(_diag)/jit(diagonal)/cond/branch_0_fun/gather | solution.py:60
  (137 shorter events, 57.9 us)
Async XLA Ops:
  7.2 108.5 %copy-start = (f32[1024,512]{1,0:T(8,128)S(1)}, f32[1024,512]{1,0:T(8,128)}, u32[]{:S(2)}) copy-start(f32[1024,512]{1,0:T(8,128)} %param.27) | copy-start | bytes 6291460
  10.8 7.9 %copy-start.22 = (f32[256,256]{1,0:T(8,128)S(1)}, f32[256,256]{1,0:T(8,128)}, u32[]{:S(2)}) copy-start(f32[256,256]{1,0:T(8,128)} %param.22) | copy-start | bytes 786436
  10.8 32.3 %copy-start.23 = (f32[256,256]{1,0:T(8,128)S(1)}, f32[256,256]{1,0:T(8,128)}, u32[]{:S(2)}) copy-start(f32[256,256]{1,0:T(8,128)} %param.30) | copy-start | bytes 786436
  10.8 70.1 %all-to-all-start = ((f32[16,16,4096]{2,1,0:T(8,128)}), f32[16,16,4096]{2,1,0:T(8,128)}, u32[]{:S(2)}, u32[]{:S(2)}) async-start(f32[16,16,4096]{2,1,0:T(8,128)} %stack.2), calls=%async_computation | async-start | bytes 8388608 | tf_op jit(solution)/shard_map/all_to_all | solution.py:12
  18.6 25.4 %copy-start.19 = (f32[256,256]{1,0:T(8,128)S(1)}, f32[256,256]{1,0:T(8,128)}, u32[]{:S(2)}) copy-start(f32[256,256]{1,0:T(8,128)} %param.23) | copy-start | bytes 786436
  18.6 114.9 %all-gather.5.cloned.1.call-start = ((), (), s32[]{:S(2)}) async-start(), calls=%async_computation.3 | async-start | bytes 1310720 | tf_op jit(solution)/shard_map/all_gather | solution.py:25
  22.8 46.9 %copy-start.11 = (f32[256,256]{1,0:T(8,128)}, f32[256,256]{1,0:T(8,128)S(1)}, u32[]{:S(2)}) copy-start(f32[256,256]{1,0:T(8,128)S(1)} %get-tuple-element.217) | copy-start | bytes 786436
  48.0 108.7 %copy-start.9 = (f32[256,256]{1,0:T(8,128)}, f32[256,256]{1,0:T(8,128)S(1)}, u32[]{:S(2)}) copy-start(f32[256,256]{1,0:T(8,128)S(1)} %get-tuple-element.216) | copy-start | bytes 786436
  67.8 31.9 %copy-start.14 = (f32[2,128,128]{1,2,0:T(8,128)}, f32[2,128,128]{1,2,0:T(8,128)S(1)}, u32[]{:S(2)}) copy-start(f32[2,128,128]{1,2,0:T(8,128)S(1)} %custom-call.22) | copy-start | bytes 393220
  85.0 3.8 %copy-start.17 = (f32[2,128,128]{1,2,0:T(8,128)S(1)}, f32[2,128,128]{1,2,0:T(8,128)}, u32[]{:S(2)}) copy-start(f32[2,128,128]{1,2,0:T(8,128)} %custom-call.21) | copy-start | bytes 393220
  98.7 4.8 %copy-start.1 = (f32[128,1024]{1,0:T(8,128)}, f32[128,1024]{1,0:T(8,128)S(1)}, u32[]{:S(2)}) copy-start(f32[128,1024]{1,0:T(8,128)S(1)} %fusion.10) | copy-start | bytes 1572868
  104.6 52.8 %all-to-all-start.2 = ((f32[4,256,256]{2,1,0:T(8,128)}), f32[4,256,256]{2,1,0:T(8,128)}, u32[]{:S(2)}, u32[]{:S(2)}) async-start(f32[4,256,256]{2,1,0:T(8,128)} %broadcast_in_dim.66), calls=%async_computation.2 | async-start | bytes 2097152 | tf_op jit(solution)/shard_map/all_to_all | solution.py:31
  110.6 41.2 %all-gather.7.cloned.1.call-start = ((), (), s32[]{:S(2)}) async-start(), calls=%async_computation.4 | async-start | bytes 1310720 | tf_op jit(solution)/shard_map/all_gather | solution.py:25
  133.5 5.6 %copy-start.18 = (f32[2,128,128]{1,2,0:T(8,128)S(1)}, f32[2,128,128]{1,2,0:T(8,128)}, u32[]{:S(2)}) copy-start(f32[2,128,128]{1,2,0:T(8,128)} %custom-call.21) | copy-start | bytes 393220
  134.9 4.6 %copy-start.12 = (f32[256,256]{1,0:T(8,128)S(1)}, f32[256,256]{1,0:T(8,128)}, u32[]{:S(2)}) copy-start(f32[256,256]{1,0:T(8,128)} %copy-done.11) | copy-start | bytes 786436
  140.4 14.3 %copy-start.13 = (f32[256,256]{1,0:T(8,128)S(1)}, f32[256,256]{1,0:T(8,128)}, u32[]{:S(2)}) copy-start(f32[256,256]{1,0:T(8,128)} %param.24) | copy-start | bytes 786436
  141.2 15.2 %copy-start.15 = (f32[2,128,128]{1,2,0:T(8,128)S(1)}, f32[2,128,128]{1,2,0:T(8,128)}, u32[]{:S(2)}) copy-start(f32[2,128,128]{1,2,0:T(8,128)} %copy-done.14) | copy-start | bytes 393220
  157.4 6.8 %copy-start.20 = (f32[256,256]{0,1:T(8,128)S(1)}, f32[256,256]{0,1:T(8,128)}, u32[]{:S(2)}) copy-start(f32[256,256]{0,1:T(8,128)} %copy.75) | copy-start | bytes 786436
  157.4 25.1 %all-to-all-start.1 = ((f32[4,64,1024]{2,1,0:T(8,128)}), f32[4,64,1024]{2,1,0:T(8,128)}, u32[]{:S(2)}, u32[]{:S(2)}) async-start(f32[4,64,1024]{2,1,0:T(8,128)} %bitcast.141), calls=%async_computation.1 | async-start | bytes 2097152 | tf_op jit(solution)/shard_map/all_to_all | solution.py:47
  163.3 6.2 %copy-start.16 = (f32[2,128,128]{1,2,0:T(8,128)S(1)}, f32[2,128,128]{1,2,0:T(8,128)}, u32[]{:S(2)}) copy-start(f32[2,128,128]{1,2,0:T(8,128)} %copy-done.14) | copy-start | bytes 393220
  164.2 5.7 %copy-start.10 = (f32[256,256]{1,0:T(8,128)S(1)}, f32[256,256]{1,0:T(8,128)}, u32[]{:S(2)}) copy-start(f32[256,256]{1,0:T(8,128)} %copy-done.9) | copy-start | bytes 786436
  175.0 9.5 %copy-start.6 = (f32[256,512]{1,0:T(8,128)S(1)}, f32[256,512]{1,0:T(8,128)}, u32[]{:S(2)}) copy-start(f32[256,512]{1,0:T(8,128)} %param.25) | copy-start | bytes 1572868
  175.0 9.5 %copy-start.24 = (f32[64,512]{1,0:T(8,128)S(1)}, f32[64,512]{1,0:T(8,128)}, u32[]{:S(2)}) copy-start(f32[64,512]{1,0:T(8,128)} %param.34) | copy-start | bytes 393220
  184.5 4.1 %copy-start.8 = (f32[256,512]{1,0:T(8,128)S(1)}, f32[256,512]{1,0:T(8,128)}, u32[]{:S(2)}) copy-start(f32[256,512]{1,0:T(8,128)} %param.26) | copy-start | bytes 1572868
  (7 other events, 18.1 us)
Sparse Core Ops, SparseCore 0:
  92.5 30.1 all-gather.4
  125.7 25.9 all-gather.6
